TPU v7x, 512 devices: a whole 4x8x8 slice. The times are simulated.
512 devices in a mesh: gx: 16 (over x, y_hi, core), gy: 32 (over y_lo, z).
Axes of the slice: x: 4, y: 8 (y_hi: 2, y_lo: 4; y = y_hi * 4 + y_lo), z: 8, core: 2. Of those that a mesh axis runs over, the one named last changes fastest.
Arguments:
- bond_mask: int32 [3, 256, 512, 128], P(None, 'gx', 'gy'), may hold values 0 or 1
- levels: float32 [2, 3], replicated, may hold values from 0.3 to 3
- electrode: int32 [2, 256, 512], P(None, 'gx', 'gy'), may hold values 0 or 1
- leakage: float32 [256, 512, 128], P('gx', 'gy'), may hold values from 0.05 to 0.5
- source: float32 [256, 512, 128], P('gx', 'gy'), may hold values from -72 to 72
- weight: float32 [256, 512, 128], P('gx', 'gy'), may hold values from -72 to 72
Outputs:
- potential: float32 [256, 512, 128], P('gx', 'gy')
- adjoint: float32 [256, 512, 128], P('gx', 'gy')
- sensitivity: float32 [3, 256, 512, 128], P(None, 'gx', 'gy')
All inputs are finite; a program needn't handle non-finite values. No bound on the sum of `bond_mask` or of `electrode` on one device may be relied on, other than what follows from the above.
Results may differ from a plain program's by a relative error of at most 0.0003.
Values sent between devices are 32-bit elements; how exact they have to be, the bound alone decides.
No kernel may reach another device: no remote copies, remote signals or barrier semaphores. Data moves between devices by JAX's collectives and lax.ppermute only.
A program may use at most 64 MiB of HBM per device.

v0:
```python
import jax
import jax.numpy as jnp
from jax import lax
from jax.sharding import PartitionSpec as P

ITERS = 4


def extended(block, sides, width):
    for axis, dim in sides:
        count = lax.axis_size(axis)
        forward = [(i, i + 1) for i in range(count - 1)]
        backward = [(target, source) for source, target in forward]
        low = lax.ppermute(
            lax.slice_in_dim(block, block.shape[dim] - width, None, axis=dim), axis, forward
        )
        high = lax.ppermute(lax.slice_in_dim(block, 0, width, axis=dim), axis, backward)
        block = jnp.concatenate([low, block, high], axis=dim)
    return block


def passed_along(value, axis, steps):
    count = lax.axis_size(axis)
    first, last = (max(0, -steps), min(count, count - steps))
    return lax.ppermute(value, axis, [(source, source + steps) for source in range(first, last)])


def totals(left, right):
    return jnp.sum(left * right, axis=(1, 2, 3))


def operate(fields, cond, below, diag):
    padded = extended(fields, (("gx", 1), ("gy", 2)), 1)
    up_x = padded[:, 2:, 1:-1]
    dn_x = padded[:, :-2, 1:-1]
    up_y = padded[:, 1:-1, 2:]
    dn_y = padded[:, 1:-1, :-2]
    zero_plane = jnp.zeros(fields.shape[:3] + (1,), jnp.float32)
    up_z = jnp.concatenate([fields[..., 1:], zero_plane], axis=3)
    dn_z = jnp.concatenate([zero_plane, fields[..., :-1]], axis=3)
    beside = (
        cond[0] * up_x
        + below[0] * dn_x
        + cond[1] * up_y
        + below[1] * dn_y
        + cond[2] * up_z
        + below[2] * dn_z
    )
    return diag * fields - beside


def precond_total(resid, scaled):
    return lax.psum(totals(resid, scaled), ("gx", "gy"))


def solve(rhs, cond, below, diag):
    solution = jnp.zeros_like(rhs)
    resid = rhs
    scaled = resid / diag
    direction = scaled
    norm_now = precond_total(resid, scaled)
    for step in range(ITERS):
        image = operate(direction, cond, below, diag)
        curv = lax.psum(totals(direction, image), ("gx", "gy"))
        alpha = (norm_now / curv)[:, None, None, None]
        solution = solution + alpha * direction
        resid = resid - alpha * image
        if step + 1 < ITERS:
            scaled = resid / diag
            fresh = precond_total(resid, scaled)
            direction = scaled + (fresh / norm_now)[:, None, None, None] * direction
            norm_now = fresh
    return solution


def body(bond_mask, levels, electrode, leakage, source, weight):
    cx, cy, nz = leakage.shape
    shape = (cx, cy, nz)
    row_x = lax.axis_index("gx") * cx + lax.broadcasted_iota(jnp.int32, (cx, 1, 1), 0)
    row_y = lax.axis_index("gy") * cy + lax.broadcasted_iota(jnp.int32, (1, cy, 1), 1)
    col_z = lax.broadcasted_iota(jnp.int32, (1, 1, nz), 2)
    inside = jnp.stack(
        [
            jnp.broadcast_to(row_x < cx * lax.axis_size("gx") - 1, shape),
            jnp.broadcast_to(row_y < cy * lax.axis_size("gy") - 1, shape),
            jnp.broadcast_to(col_z < nz - 1, shape),
        ]
    ).astype(jnp.float32)
    cond = (
        jnp.where(bond_mask == 1, levels[1][:, None, None, None], levels[0][:, None, None, None])
        * inside
    )
    rim_x = passed_along(cond[0, -1:], "gx", 1)
    rim_y = passed_along(cond[1, :, -1:], "gy", 1)
    below_x = jnp.concatenate([rim_x, cond[0, :-1]], axis=0)
    below_y = jnp.concatenate([rim_y, cond[1, :, :-1]], axis=1)
    below_z = jnp.concatenate([jnp.zeros((cx, cy, 1), jnp.float32), cond[2, :, :, :-1]], axis=2)
    below = (below_x, below_y, below_z)
    elec = electrode.astype(jnp.float32)
    first = jnp.where(col_z == 0, elec[0][:, :, None], 0.0)
    last = jnp.where(col_z == nz - 1, elec[1][:, :, None], 0.0)
    diag = leakage + first + last + cond[0] + cond[1] + cond[2] + below_x + below_y + below_z
    rhs = jnp.stack([source + first, weight + last])
    fields = jnp.concatenate(
        [solve(rhs[0:1], cond, below, diag), solve(rhs[1:2], cond, below, diag)], axis=0
    )
    next_x = passed_along(fields[:, :1], "gx", -1)
    next_y = passed_along(fields[:, :, :1], "gy", -1)
    up_x = jnp.concatenate([fields[:, 1:], next_x], axis=1)
    up_y = jnp.concatenate([fields[:, :, 1:], next_y], axis=2)
    up_z = jnp.concatenate([fields[..., 1:], jnp.zeros((2, cx, cy, 1), jnp.float32)], axis=3)
    potential = fields[0]
    adjoint = fields[1]
    sens = jnp.stack(
        [
            -(adjoint - ups[1]) * (potential - ups[0]) * inside[d]
            for d, ups in enumerate((up_x, up_y, up_z))
        ]
    )
    return (potential, adjoint, sens)


def solution(mesh):
    return jax.shard_map(
        body,
        mesh=mesh,
        in_specs=(
            P(None, "gx", "gy", None),
            P(),
            P(None, "gx", "gy"),
            P("gx", "gy", None),
            P("gx", "gy", None),
            P("gx", "gy", None),
        ),
        out_specs=(P("gx", "gy", None), P("gx", "gy", None), P(None, "gx", "gy", None)),
        check_vma=False,
    )
```

profile of v0, /device:TPU:1, one launch (start us, length us, event | category | flops | bytes accessed | tf_op | source)
XLA Modules:
  0.0 1077.7 jit_solution(148761444872244542)
XLA Ops:
  1.5 1.1 select_select_fusion
  2.7 8.8 collective-permute-start
  11.6 4.0 collective-permute-start.1
  16.6 0.8 multiply_reduce_fusion.13
  18.3 3.8 collective-permute-start.19
  22.2 1.9 collective-permute-start.18
  24.2 7.5 collective-permute-start.3
  31.7 1.9 collective-permute-start.2
  33.7 1.3 collective-permute-start.20
  35.0 4.6 collective-permute-start.21
  39.7 1.0 collective-permute-done.2
  40.6 1.3 collective-permute-start.4
  41.9 4.6 collective-permute-start.5
  46.6 0.8 multiply_reduce_fusion.5
  47.4 108.5 %all-reduce.23 = (f32[1]{0:T(128)}, f32[1]{0:T(128)}) all-reduce(f32[1]{0:T(128)} %bitcast.37, f32[1]{0:T(128)} %bitcast.40), channel_id=1, replica_groups=mesh['gx'=16,'gy'=32] {'gx','gy'}, use_global_device_ids=true, to_apply=%region_17.18 | all-reduce | flops 2 | bytes 16 | tf_op jit(solution)/shard_map/psum | solution.py:53
  157.2 0.8 multiply_reduce_fusion.4
  158.0 93.5 %psum.122 = f32[1]{0:T(128)} all-reduce(f32[1]{0:T(128)} %bitcast.44), channel_id=1, replica_groups=mesh['gx'=16,'gy'=32] {'gx','gy'}, use_global_device_ids=true, to_apply=%region_21.22 | all-reduce | flops 1 | bytes 8 | tf_op jit(solution)/shard_map/psum | solution.py:53
  252.9 6.1 collective-permute-start.23
  259.0 1.9 collective-permute-start.22
  261.0 0.8 multiply_reduce_fusion.12
  261.8 6.1 collective-permute-done.22
  267.9 1.3 collective-permute-start.24
  269.2 4.0 collective-permute-start.25
  274.0 0.8 multiply_reduce_fusion.3
  274.8 98.8 %all-reduce.22 = (f32[1]{0:T(128)}, f32[1]{0:T(128)}, f32[1]{0:T(128)}) all-reduce(f32[1]{0:T(128)} %bitcast.47, f32[1]{0:T(128)} %bitcast.12, f32[1]{0:T(128)} %bitcast.18), channel_id=1, replica_groups=mesh['gx'=16,'gy'=32] {'gx','gy'}, use_global_device_ids=true, to_apply=%region_23.24 | all-reduce | flops 3 | bytes 24 | tf_op jit(solution)/shard_map/psum | solution.py:64
  376.2 0.7 multiply_reduce_fusion.2
  377.0 95.3 %all-reduce.21 = (f32[1]{0:T(128)}, f32[1]{0:T(128)}) all-reduce(f32[1]{0:T(128)} %bitcast.23, f32[1]{0:T(128)} %bitcast.49), channel_id=1, replica_groups=mesh['gx'=16,'gy'=32] {'gx','gy'}, use_global_device_ids=true, to_apply=%region_5.6 | all-reduce | flops 2 | bytes 16 | tf_op jit(solution)/shard_map/psum | solution.py:53
  475.0 5.3 collective-permute-start.27
  480.4 1.9 collective-permute-start.26
  482.4 7.5 collective-permute-start.7
  490.0 1.9 collective-permute-start.6
  491.9 1.3 collective-permute-start.28
  493.2 4.0 collective-permute-start.29
  497.2 1.6 collective-permute-done.6
  498.9 1.3 collective-permute-start.8
  500.2 4.0 collective-permute-start.9
  504.2 0.8 multiply_reduce_fusion.1
  504.9 0.8 multiply_reduce_fusion.10
  505.7 104.2 %all-reduce.20 = (f32[1]{0:T(128)}, f32[1]{0:T(128)}) all-reduce(f32[1]{0:T(128)} %bitcast.51, f32[1]{0:T(128)} %bitcast.26), channel_id=1, replica_groups=mesh['gx'=16,'gy'=32] {'gx','gy'}, use_global_device_ids=true, to_apply=%region_27.28 | all-reduce | flops 2 | bytes 16 | tf_op jit(solution)/shard_map/psum | solution.py:64
  613.2 93.5 %psum.116 = f32[1]{0:T(128)} all-reduce(f32[1]{0:T(128)} %bitcast.28), channel_id=1, replica_groups=mesh['gx'=16,'gy'=32] {'gx','gy'}, use_global_device_ids=true, to_apply=%region_9.10 | all-reduce | flops 1 | bytes 8 | tf_op jit(solution)/shard_map/psum | solution.py:53
  708.2 6.5 collective-permute-start.11
  714.7 1.9 collective-permute-start.10
  716.7 6.9 collective-permute-done.10
  723.6 1.3 collective-permute-start.12
  724.9 4.0 collective-permute-start.13
  729.7 0.8 multiply_reduce_fusion.8
  730.6 98.3 %psum.117 = f32[1]{0:T(128)} all-reduce(f32[1]{0:T(128)} %bitcast.30), channel_id=1, replica_groups=mesh['gx'=16,'gy'=32] {'gx','gy'}, use_global_device_ids=true, to_apply=%region_11.12 | all-reduce | flops 1 | bytes 8 | tf_op jit(solution)/shard_map/psum | solution.py:64
  830.9 95.1 %all-reduce.19 = (f32[1]{0:T(128)}, f32[1]{0:T(128)}) all-reduce(f32[1]{0:T(128)} %bitcast.32, f32[1]{0:T(128)} %bitcast.53), channel_id=1, replica_groups=mesh['gx'=16,'gy'=32] {'gx','gy'}, use_global_device_ids=true, to_apply=%region_13.14 | all-reduce | flops 2 | bytes 16 | tf_op jit(solution)/shard_map/psum | solution.py:53
  928.7 5.4 collective-permute-start.31
  934.1 1.9 collective-permute-start.30
  936.2 7.5 collective-permute-start.15
  943.7 1.9 collective-permute-start.14
  945.7 1.3 collective-permute-start.32
  947.0 4.0 collective-permute-start.33
  951.0 1.6 collective-permute-done.14
  952.6 1.3 collective-permute-start.16
  953.9 4.0 collective-permute-start.17
  957.9 0.8 fusion.28
  958.7 0.7 fusion.70
  959.5 104.1 %all-reduce.18 = (f32[1]{0:T(128)}, f32[1]{0:T(128)}) all-reduce(f32[1]{0:T(128)} %bitcast.34, f32[1]{0:T(128)} %bitcast.55), channel_id=1, replica_groups=mesh['gx'=16,'gy'=32] {'gx','gy'}, use_global_device_ids=true, to_apply=%region_15.16 | all-reduce | flops 2 | bytes 16 | tf_op jit(solution)/shard_map/psum | solution.py:64
  1066.5 1.3 collective-permute-start.35
  1067.8 2.6 collective-permute-start.34
  1071.0 5.8 collective-permute-done.34
  1076.9 0.8 pad_maximum_fusion
  (99 shorter events, 7.5 us)
Async XLA Ops:
  0.7 0.7 copy-start.6
  2.7 13.6 %collective-permute-start = (f32[1,16,128]{2,1,0:T(8,128)S(1)}, f32[1,16,128]{2,1,0:T(8,128)S(1)}, u32[]{:S(2)}, u32[]{:S(2)}) collective-permute-start(f32[1,16,128]{2,1,0:T(8,128)S(1)} %slice_bitcast_fusion.4), channel_id=1, source_target_pairs={{0,32},{32,64},{64,96},{96,128},{128,160},{160,192},{192,224},{224... | collective-permute-start | bytes 24584 | tf_op jit(solution)/shard_map/ppermute | solution.py:25
  11.6 4.8 collective-permute-start.1
  15.6 0.7 copy-start.5
  15.6 0.9 copy-start.3
  15.6 1.0 copy-start.4
  16.6 0.9 copy-start.2
  18.3 15.4 %collective-permute-start.19 = (f32[1,1,16,128]{3,2,1,0:T(8,128)S(1)}, f32[1,1,16,128]{3,2,1,0:T(8,128)S(1)}, u32[]{:S(2)}, u32[]{:S(2)}) collective-permute-start(f32[1,1,16,128]{3,2,1,0:T(8,128)S(1)} %get-tuple-element.89), channel_id=1, source_target_pairs={{0,32},{32,64},{64,96},{96,128},{128,160},{160,192},{192,224},{224... | collective-permute-start | bytes 24584 | tf_op jit(solution)/shard_map/ppermute | solution.py:14
  22.2 11.5 %collective-permute-start.18 = (f32[1,1,16,128]{3,2,1,0:T(8,128)S(1)}, f32[1,1,16,128]{3,2,1,0:T(8,128)S(1)}, u32[]{:S(2)}, u32[]{:S(2)}) collective-permute-start(f32[1,1,16,128]{3,2,1,0:T(8,128)S(1)} %get-tuple-element.90), channel_id=1, source_target_pairs={{32,0},{64,32},{96,64},{128,96},{160,128},{192,160},{224,192},{256... | collective-permute-start | bytes 24584 | tf_op jit(solution)/shard_map/ppermute | solution.py:17
  24.2 15.5 %collective-permute-start.3 = (f32[1,1,16,128]{3,2,1,0:T(8,128)S(1)}, f32[1,1,16,128]{3,2,1,0:T(8,128)S(1)}, u32[]{:S(2)}, u32[]{:S(2)}) collective-permute-start(f32[1,1,16,128]{3,2,1,0:T(8,128)S(1)} %get-tuple-element.93), channel_id=1, source_target_pairs={{0,32},{32,64},{64,96},{96,128},{128,160},{160,192},{192,224},{224... | collective-permute-start | bytes 24584 | tf_op jit(solution)/shard_map/ppermute | solution.py:14
  31.7 8.9 collective-permute-start.2
  33.7 12.9 %collective-permute-start.20 = (f32[1,18,1,128]{3,2,1,0:T(1,128)S(1)}, f32[1,18,1,128]{3,2,1,0:T(1,128)S(1)}, u32[]{:S(2)}, u32[]{:S(2)}) collective-permute-start(f32[1,18,1,128]{3,2,1,0:T(1,128)S(1)} %get-tuple-element.57), channel_id=1, source_target_pairs={{1,0},{2,1},{3,2},{4,3},{5,4},{6,5},{7,6},{8,7},{9,8},{10,9},{11,1... | collective-permute-start | bytes 27656 | tf_op jit(solution)/shard_map/ppermute | solution.py:17
  35.0 11.6 %collective-permute-start.21 = (f32[1,18,1,128]{3,2,1,0:T(1,128)S(1)}, f32[1,18,1,128]{3,2,1,0:T(1,128)S(1)}, u32[]{:S(2)}, u32[]{:S(2)}) collective-permute-start(f32[1,18,1,128]{3,2,1,0:T(1,128)S(1)} %get-tuple-element.58), channel_id=1, source_target_pairs={{0,1},{1,2},{2,3},{3,4},{4,5},{5,6},{6,7},{7,8},{8,9},{9,10},{10,1... | collective-permute-start | bytes 27656 | tf_op jit(solution)/shard_map/ppermute | solution.py:14
  40.6 220.3 %collective-permute-start.4 = (f32[1,18,1,128]{3,2,1,0:T(1,128)S(1)}, f32[1,18,1,128]{3,2,1,0:T(1,128)S(1)}, u32[]{:S(2)}, u32[]{:S(2)}) collective-permute-start(f32[1,18,1,128]{3,2,1,0:T(1,128)S(1)} %get-tuple-element.59), channel_id=1, source_target_pairs={{1,0},{2,1},{3,2},{4,3},{5,4},{6,5},{7,6},{8,7},{9,8},{10,9},{11,1... | collective-permute-start | bytes 27656 | tf_op jit(solution)/shard_map/ppermute | solution.py:17
  41.9 219.0 %collective-permute-start.5 = (f32[1,18,1,128]{3,2,1,0:T(1,128)S(1)}, f32[1,18,1,128]{3,2,1,0:T(1,128)S(1)}, u32[]{:S(2)}, u32[]{:S(2)}) collective-permute-start(f32[1,18,1,128]{3,2,1,0:T(1,128)S(1)} %get-tuple-element.60), channel_id=1, source_target_pairs={{0,1},{1,2},{2,3},{3,4},{4,5},{5,6},{6,7},{7,8},{8,9},{9,10},{10,1... | collective-permute-start | bytes 27656 | tf_op jit(solution)/shard_map/ppermute | solution.py:14
  252.9 8.9 collective-permute-start.23
  259.0 8.9 collective-permute-start.22
  267.9 5.4 collective-permute-start.24
  269.2 4.8 collective-permute-start.25
  475.0 16.9 %collective-permute-start.27 = (f32[1,1,16,128]{3,2,1,0:T(8,128)S(1)}, f32[1,1,16,128]{3,2,1,0:T(8,128)S(1)}, u32[]{:S(2)}, u32[]{:S(2)}) collective-permute-start(f32[1,1,16,128]{3,2,1,0:T(8,128)S(1)} %get-tuple-element.79), channel_id=1, source_target_pairs={{0,32},{32,64},{64,96},{96,128},{128,160},{160,192},{192,224},{224... | collective-permute-start | bytes 24584 | tf_op jit(solution)/shard_map/ppermute | solution.py:14
  480.4 11.5 %collective-permute-start.26 = (f32[1,1,16,128]{3,2,1,0:T(8,128)S(1)}, f32[1,1,16,128]{3,2,1,0:T(8,128)S(1)}, u32[]{:S(2)}, u32[]{:S(2)}) collective-permute-start(f32[1,1,16,128]{3,2,1,0:T(8,128)S(1)} %get-tuple-element.80), channel_id=1, source_target_pairs={{32,0},{64,32},{96,64},{128,96},{160,128},{192,160},{224,192},{256... | collective-permute-start | bytes 24584 | tf_op jit(solution)/shard_map/ppermute | solution.py:17
  482.4 14.8 %collective-permute-start.7 = (f32[1,1,16,128]{3,2,1,0:T(8,128)S(1)}, f32[1,1,16,128]{3,2,1,0:T(8,128)S(1)}, u32[]{:S(2)}, u32[]{:S(2)}) collective-permute-start(f32[1,1,16,128]{3,2,1,0:T(8,128)S(1)} %get-tuple-element.75), channel_id=1, source_target_pairs={{0,32},{32,64},{64,96},{96,128},{128,160},{160,192},{192,224},{224... | collective-permute-start | bytes 24584 | tf_op jit(solution)/shard_map/ppermute | solution.py:14
  490.0 8.9 collective-permute-start.6
  491.9 12.2 %collective-permute-start.28 = (f32[1,18,1,128]{3,2,1,0:T(1,128)S(1)}, f32[1,18,1,128]{3,2,1,0:T(1,128)S(1)}, u32[]{:S(2)}, u32[]{:S(2)}) collective-permute-start(f32[1,18,1,128]{3,2,1,0:T(1,128)S(1)} %get-tuple-element.53), channel_id=1, source_target_pairs={{1,0},{2,1},{3,2},{4,3},{5,4},{6,5},{7,6},{8,7},{9,8},{10,9},{11,1... | collective-permute-start | bytes 27656 | tf_op jit(solution)/shard_map/ppermute | solution.py:17
  493.2 10.9 %collective-permute-start.29 = (f32[1,18,1,128]{3,2,1,0:T(1,128)S(1)}, f32[1,18,1,128]{3,2,1,0:T(1,128)S(1)}, u32[]{:S(2)}, u32[]{:S(2)}) collective-permute-start(f32[1,18,1,128]{3,2,1,0:T(1,128)S(1)} %get-tuple-element.54), channel_id=1, source_target_pairs={{0,1},{1,2},{2,3},{3,4},{4,5},{5,6},{6,7},{7,8},{8,9},{9,10},{10,1... | collective-permute-start | bytes 27656 | tf_op jit(solution)/shard_map/ppermute | solution.py:14
  498.9 6.1 collective-permute-start.8
  500.2 4.8 collective-permute-start.9
  708.2 8.5 collective-permute-start.11
  714.7 8.9 collective-permute-start.10
  723.6 5.4 collective-permute-start.12
  724.9 4.8 collective-permute-start.13
  928.7 16.9 %collective-permute-start.31 = (f32[1,1,16,128]{3,2,1,0:T(8,128)S(1)}, f32[1,1,16,128]{3,2,1,0:T(8,128)S(1)}, u32[]{:S(2)}, u32[]{:S(2)}) collective-permute-start(f32[1,1,16,128]{3,2,1,0:T(8,128)S(1)} %get-tuple-element.63), channel_id=1, source_target_pairs={{0,32},{32,64},{64,96},{96,128},{128,160},{160,192},{192,224},{224... | collective-permute-start | bytes 24584 | tf_op jit(solution)/shard_map/ppermute | solution.py:14
  934.1 11.5 %collective-permute-start.30 = (f32[1,1,16,128]{3,2,1,0:T(8,128)S(1)}, f32[1,1,16,128]{3,2,1,0:T(8,128)S(1)}, u32[]{:S(2)}, u32[]{:S(2)}) collective-permute-start(f32[1,1,16,128]{3,2,1,0:T(8,128)S(1)} %get-tuple-element.64), channel_id=1, source_target_pairs={{32,0},{64,32},{96,64},{128,96},{160,128},{192,160},{224,192},{256... | collective-permute-start | bytes 24584 | tf_op jit(solution)/shard_map/ppermute | solution.py:17
  936.2 14.8 %collective-permute-start.15 = (f32[1,1,16,128]{3,2,1,0:T(8,128)S(1)}, f32[1,1,16,128]{3,2,1,0:T(8,128)S(1)}, u32[]{:S(2)}, u32[]{:S(2)}) collective-permute-start(f32[1,1,16,128]{3,2,1,0:T(8,128)S(1)} %get-tuple-element.69), channel_id=1, source_target_pairs={{0,32},{32,64},{64,96},{96,128},{128,160},{160,192},{192,224},{224... | collective-permute-start | bytes 24584 | tf_op jit(solution)/shard_map/ppermute | solution.py:14
  943.7 8.9 collective-permute-start.14
  945.7 12.2 %collective-permute-start.32 = (f32[1,18,1,128]{3,2,1,0:T(1,128)S(1)}, f32[1,18,1,128]{3,2,1,0:T(1,128)S(1)}, u32[]{:S(2)}, u32[]{:S(2)}) collective-permute-start(f32[1,18,1,128]{3,2,1,0:T(1,128)S(1)} %get-tuple-element.45), channel_id=1, source_target_pairs={{1,0},{2,1},{3,2},{4,3},{5,4},{6,5},{7,6},{8,7},{9,8},{10,9},{11,1... | collective-permute-start | bytes 27656 | tf_op jit(solution)/shard_map/ppermute | solution.py:17
  947.0 10.9 %collective-permute-start.33 = (f32[1,18,1,128]{3,2,1,0:T(1,128)S(1)}, f32[1,18,1,128]{3,2,1,0:T(1,128)S(1)}, u32[]{:S(2)}, u32[]{:S(2)}) collective-permute-start(f32[1,18,1,128]{3,2,1,0:T(1,128)S(1)} %get-tuple-element.46), channel_id=1, source_target_pairs={{0,1},{1,2},{2,3},{3,4},{4,5},{5,6},{6,7},{7,8},{8,9},{9,10},{10,1... | collective-permute-start | bytes 27656 | tf_op jit(solution)/shard_map/ppermute | solution.py:14
  952.6 6.1 collective-permute-start.16
  953.9 4.8 collective-permute-start.17
  1066.2 10.6 copy-start
  1066.3 10.5 copy-start.1
  1066.5 4.5 collective-permute-start.35
  1067.8 9.0 collective-permute-start.34
where the time goes:
time: 1080 us
  blocking collectives  891 us (82%)
  starting transfers between devices  125 us (12%)
  waiting for transfers between devices  25 us (2%)
  between operations  19.9 us (2%)
  other arithmetic  13.4 us (1%)
    psum x5, blocking collectives, precond_total(): return lax.psum(totals(resid, scaled), ('gx', 'gy'))  486 us
    psum x4, blocking collectives, solve(): curv = lax.psum(totals(direction, image), ('gx', 'gy'))  405 us
    ppermute x16, starting transfers between devices, extended(): lax.ppermute(lax.slice_in_dim(block, block.shape[dim] - width, None, axis...  83 us
    ppermute x16, starting transfers between devices, extended(): lax.ppermute(lax.slice_in_dim(block, 0, width, axis=dim), axis, backward)  25.7 us
  transfers between devices with their start and end apart: 36, of which 9 were waited for; matrix products, arithmetic and copies ran while one was open for 0% of the time, Pallas kernels for 0%

commit v1 on v0

--- a/solution.py
+++ b/solution.py
@@ -61,7 +61,7 @@
     norm_now = precond_total(resid, scaled)
     for step in range(ITERS):
         image = operate(direction, cond, below, diag)
-        curv = lax.psum(totals(direction, image), ("gx", "gy"))
+        curv = lax.psum(lax.psum(totals(direction, image), "gy"), "gx")
         alpha = (norm_now / curv)[:, None, None, None]
         solution = solution + alpha * direction
         resid = resid - alpha * image

time: 1080 us -> 1260 us (1.17)
  blocking collectives: 891 us -> 1080 us
    psum x4 -> x10, blocking collectives: 405 us -> 595 us  [solve(): curv = lax.psum(lax.psum(totals(direction, image), 'gy'), 'gx')]
  transfers between devices with their start and end apart: 36 -> 36, of which waited for: 9 -> 8; matrix products, arithmetic and copies ran while one was open for 0% -> 0% of each run, Pallas kernels for 0% -> 0%
where the time goes in v1:
time: 1260 us; the launch traced here: 1250 us
  blocking collectives  1080 us (86%)
  starting transfers between devices  117 us (9%)
  waiting for transfers between devices  24.6 us (2%)
  between operations  19.4 us (2%)
  other arithmetic  13.2 us (1%)
    psum x10, blocking collectives, solve(): curv = lax.psum(lax.psum(totals(direction, image), 'gy'), 'gx')  595 us
    psum x5, blocking collectives, precond_total(): return lax.psum(totals(resid, scaled), ('gx', 'gy'))  481 us
    ppermute x16, starting transfers between devices, extended(): lax.ppermute(lax.slice_in_dim(block, block.shape[dim] - width, None, axis...  74.8 us
    ppermute x16, starting transfers between devices, extended(): lax.ppermute(lax.slice_in_dim(block, 0, width, axis=dim), axis, backward)  25.7 us
  transfers between devices with their start and end apart: 36, of which 8 were waited for; matrix products, arithmetic and copies ran while one was open for 0% of the time, Pallas kernels for 0%

profile of v1, /device:TPU:1, one launch (start us, length us, event | category | flops | bytes accessed | tf_op | source)
XLA Modules:
  0.0 1253.1 jit_solution(7940689306928079018)
XLA Ops:
  1.5 1.1 select_select_fusion
  2.7 8.8 collective-permute-start
  11.6 4.0 collective-permute-start.1
  16.6 0.8 multiply_reduce_fusion.13
  18.3 3.8 collective-permute-start.19
  22.2 1.9 collective-permute-start.18
  24.2 7.5 collective-permute-start.3
  31.7 1.9 collective-permute-start.2
  33.7 105.4 %psum.180 = f32[1]{0:T(128)} all-reduce(f32[1]{0:T(128)} %bitcast.37), channel_id=1, replica_groups=mesh['gx'=16,'gy'=32] {'gx','gy'}, use_global_device_ids=true, to_apply=%region_21.22 | all-reduce | flops 1 | bytes 8 | tf_op jit(solution)/shard_map/psum | solution.py:53
  139.1 1.3 collective-permute-start.20
  140.4 4.0 collective-permute-start.21
  144.4 1.3 collective-permute-start.4
  145.7 0.8 multiply_reduce_fusion.5
  146.5 65.1 %psum.181 = f32[1]{0:T(128)} all-reduce(f32[1]{0:T(128)} %bitcast.40), channel_id=1, replica_groups=mesh['gx'=16,'gy'=32] {'gy'}, use_global_device_ids=true, to_apply=%region_23.24 | all-reduce | flops 1 | bytes 8 | tf_op jit(solution)/shard_map/psum | solution.py:64
  211.6 1.3 collective-permute-start.5
  212.9 58.0 %psum.182 = f32[1]{0:T(128)} all-reduce(f32[1]{0:T(128)} %psum.181), channel_id=1, replica_groups=mesh['gx'=16,'gy'=32] {'gx'}, use_global_device_ids=true, to_apply=%region_24.25 | all-reduce | flops 1 | bytes 8 | tf_op jit(solution)/shard_map/psum | solution.py:64
  272.9 93.6 %all-reduce.20 = (f32[1]{0:T(128)}, f32[1]{0:T(128)}) all-reduce(f32[1]{0:T(128)} %bitcast.44, f32[1]{0:T(128)} %bitcast.12), channel_id=1, replica_groups=mesh['gx'=16,'gy'=32] {'gx','gy'}, use_global_device_ids=true, to_apply=%region_26.27 | all-reduce | flops 2 | bytes 16 | tf_op jit(solution)/shard_map/psum | solution.py:53
  367.9 4.6 collective-permute-start.23
  372.5 1.9 collective-permute-start.22
  374.5 0.8 multiply_reduce_fusion.12
  375.2 6.1 collective-permute-done.22
  381.4 1.3 collective-permute-start.24
  382.7 4.0 collective-permute-start.25
  387.5 0.8 multiply_reduce_fusion.3
  388.3 63.7 %all-reduce.23 = (f32[1]{0:T(128)}, f32[1]{0:T(128)}) all-reduce(f32[1]{0:T(128)} %bitcast.47, f32[1]{0:T(128)} %bitcast.18), channel_id=1, replica_groups=mesh['gx'=16,'gy'=32] {'gy'}, use_global_device_ids=true, to_apply=%region_28.29 | all-reduce | flops 2 | bytes 16 | tf_op jit(solution)/shard_map/psum | solution.py:64
  452.0 52.3 %all-reduce.26 = (f32[1]{0:T(128)}, f32[1]{0:T(128)}) all-reduce(f32[1]{0:T(128)} %get-tuple-element.17, f32[1]{0:T(128)} %get-tuple-element.18), channel_id=1, replica_groups=mesh['gx'=16,'gy'=32] {'gx'}, use_global_device_ids=true, to_apply=%region_29.30 | all-reduce | flops 2 | bytes 16 | tf_op jit(solution)/shard_map/psum | solution.py:64
  507.7 94.1 %all-reduce.19 = (f32[1]{0:T(128)}, f32[1]{0:T(128)}) all-reduce(f32[1]{0:T(128)} %bitcast.23, f32[1]{0:T(128)} %bitcast.49), channel_id=1, replica_groups=mesh['gx'=16,'gy'=32] {'gx','gy'}, use_global_device_ids=true, to_apply=%region_6.7 | all-reduce | flops 2 | bytes 16 | tf_op jit(solution)/shard_map/psum | solution.py:53
  604.6 4.6 collective-permute-start.27
  609.2 1.9 collective-permute-start.26
  611.2 7.5 collective-permute-start.7
  618.8 1.9 collective-permute-start.6
  620.8 1.3 collective-permute-start.28
  622.1 4.0 collective-permute-start.29
  626.1 1.6 collective-permute-done.6
  627.7 1.3 collective-permute-start.8
  629.0 4.0 collective-permute-start.9
  634.5 63.2 %all-reduce.22 = (f32[1]{0:T(128)}, f32[1]{0:T(128)}) all-reduce(f32[1]{0:T(128)} %bitcast.51, f32[1]{0:T(128)} %bitcast.26), channel_id=1, replica_groups=mesh['gx'=16,'gy'=32] {'gy'}, use_global_device_ids=true, to_apply=%region_33.34 | all-reduce | flops 2 | bytes 16 | tf_op jit(solution)/shard_map/psum | solution.py:64
  697.7 56.8 %all-reduce.25 = (f32[1]{0:T(128)}, f32[1]{0:T(128)}) all-reduce(f32[1]{0:T(128)} %get-tuple-element.15, f32[1]{0:T(128)} %get-tuple-element.16), channel_id=1, replica_groups=mesh['gx'=16,'gy'=32] {'gx'}, use_global_device_ids=true, to_apply=%region_34.35 | all-reduce | flops 2 | bytes 16 | tf_op jit(solution)/shard_map/psum | solution.py:64
  757.9 94.8 %psum.174 = f32[1]{0:T(128)} all-reduce(f32[1]{0:T(128)} %bitcast.28), channel_id=1, replica_groups=mesh['gx'=16,'gy'=32] {'gx','gy'}, use_global_device_ids=true, to_apply=%region_11.12 | all-reduce | flops 1 | bytes 8 | tf_op jit(solution)/shard_map/psum | solution.py:53
  853.9 5.0 collective-permute-start.11
  858.9 1.9 collective-permute-start.10
  860.8 6.9 collective-permute-done.10
  867.8 1.3 collective-permute-start.12
  869.1 4.0 collective-permute-start.13
  873.9 0.8 multiply_reduce_fusion.8
  874.6 63.6 %psum.175 = f32[1]{0:T(128)} all-reduce(f32[1]{0:T(128)} %bitcast.30), channel_id=1, replica_groups=mesh['gx'=16,'gy'=32] {'gy'}, use_global_device_ids=true, to_apply=%region_13.14 | all-reduce | flops 1 | bytes 8 | tf_op jit(solution)/shard_map/psum | solution.py:64
  938.3 52.2 %psum.176 = f32[1]{0:T(128)} all-reduce(f32[1]{0:T(128)} %psum.175), channel_id=1, replica_groups=mesh['gx'=16,'gy'=32] {'gx'}, use_global_device_ids=true, to_apply=%region_14.15 | all-reduce | flops 1 | bytes 8 | tf_op jit(solution)/shard_map/psum | solution.py:64
  992.4 93.6 %all-reduce.18 = (f32[1]{0:T(128)}, f32[1]{0:T(128)}) all-reduce(f32[1]{0:T(128)} %bitcast.32, f32[1]{0:T(128)} %bitcast.53), channel_id=1, replica_groups=mesh['gx'=16,'gy'=32] {'gx','gy'}, use_global_device_ids=true, to_apply=%region_16.17 | all-reduce | flops 2 | bytes 16 | tf_op jit(solution)/shard_map/psum | solution.py:53
  1088.7 5.0 collective-permute-start.31
  1093.7 1.9 collective-permute-start.30
  1095.7 7.5 collective-permute-start.15
  1103.3 1.9 collective-permute-start.14
  1105.3 1.3 collective-permute-start.32
  1106.6 4.0 collective-permute-start.33
  1110.6 1.6 collective-permute-done.14
  1112.2 1.3 collective-permute-start.16
  1113.5 4.0 collective-permute-start.17
  1119.0 63.2 %all-reduce.21 = (f32[1]{0:T(128)}, f32[1]{0:T(128)}) all-reduce(f32[1]{0:T(128)} %bitcast.34, f32[1]{0:T(128)} %bitcast.55), channel_id=1, replica_groups=mesh['gx'=16,'gy'=32] {'gy'}, use_global_device_ids=true, to_apply=%region_18.19 | all-reduce | flops 2 | bytes 16 | tf_op jit(solution)/shard_map/psum | solution.py:64
  1182.2 56.9 %all-reduce.24 = (f32[1]{0:T(128)}, f32[1]{0:T(128)}) all-reduce(f32[1]{0:T(128)} %get-tuple-element.13, f32[1]{0:T(128)} %get-tuple-element.14), channel_id=1, replica_groups=mesh['gx'=16,'gy'=32] {'gx'}, use_global_device_ids=true, to_apply=%region_19.20 | all-reduce | flops 2 | bytes 16 | tf_op jit(solution)/shard_map/psum | solution.py:64
  1241.9 1.3 collective-permute-start.35
  1243.2 2.1 collective-permute-start.34
  1245.3 1.1 collective-permute-done.35
  1246.4 5.8 collective-permute-done.34
  1252.3 0.8 pad_maximum_fusion
  (105 shorter events, 11.5 us)
Async XLA Ops:
  0.7 0.7 copy-start.6
  2.7 13.6 %collective-permute-start = (f32[1,16,128]{2,1,0:T(8,128)S(1)}, f32[1,16,128]{2,1,0:T(8,128)S(1)}, u32[]{:S(2)}, u32[]{:S(2)}) collective-permute-start(f32[1,16,128]{2,1,0:T(8,128)S(1)} %slice_bitcast_fusion.4), channel_id=1, source_target_pairs={{0,32},{32,64},{64,96},{96,128},{128,160},{160,192},{192,224},{224... | collective-permute-start | bytes 24584 | tf_op jit(solution)/shard_map/ppermute | solution.py:25
  11.6 4.8 collective-permute-start.1
  15.6 0.7 copy-start.5
  15.6 0.9 copy-start.3
  15.6 1.0 copy-start.4
  16.6 0.9 copy-start.2
  18.3 120.8 %collective-permute-start.19 = (f32[1,1,16,128]{3,2,1,0:T(8,128)S(1)}, f32[1,1,16,128]{3,2,1,0:T(8,128)S(1)}, u32[]{:S(2)}, u32[]{:S(2)}) collective-permute-start(f32[1,1,16,128]{3,2,1,0:T(8,128)S(1)} %get-tuple-element.94), channel_id=1, source_target_pairs={{0,32},{32,64},{64,96},{96,128},{128,160},{160,192},{192,224},{224... | collective-permute-start | bytes 24584 | tf_op jit(solution)/shard_map/ppermute | solution.py:14
  22.2 116.9 %collective-permute-start.18 = (f32[1,1,16,128]{3,2,1,0:T(8,128)S(1)}, f32[1,1,16,128]{3,2,1,0:T(8,128)S(1)}, u32[]{:S(2)}, u32[]{:S(2)}) collective-permute-start(f32[1,1,16,128]{3,2,1,0:T(8,128)S(1)} %get-tuple-element.95), channel_id=1, source_target_pairs={{32,0},{64,32},{96,64},{128,96},{160,128},{192,160},{224,192},{256... | collective-permute-start | bytes 24584 | tf_op jit(solution)/shard_map/ppermute | solution.py:17
  24.2 120.2 %collective-permute-start.3 = (f32[1,1,16,128]{3,2,1,0:T(8,128)S(1)}, f32[1,1,16,128]{3,2,1,0:T(8,128)S(1)}, u32[]{:S(2)}, u32[]{:S(2)}) collective-permute-start(f32[1,1,16,128]{3,2,1,0:T(8,128)S(1)} %get-tuple-element.98), channel_id=1, source_target_pairs={{0,32},{32,64},{64,96},{96,128},{128,160},{160,192},{192,224},{224... | collective-permute-start | bytes 24584 | tf_op jit(solution)/shard_map/ppermute | solution.py:14
  31.7 112.6 %collective-permute-start.2 = (f32[1,1,16,128]{3,2,1,0:T(8,128)S(1)}, f32[1,1,16,128]{3,2,1,0:T(8,128)S(1)}, u32[]{:S(2)}, u32[]{:S(2)}) collective-permute-start(f32[1,1,16,128]{3,2,1,0:T(8,128)S(1)} %get-tuple-element.99), channel_id=1, source_target_pairs={{32,0},{64,32},{96,64},{128,96},{160,128},{192,160},{224,192},{256... | collective-permute-start | bytes 24584 | tf_op jit(solution)/shard_map/ppermute | solution.py:17
  139.1 6.6 collective-permute-start.20
  140.4 5.4 collective-permute-start.21
  144.4 230.0 %collective-permute-start.4 = (f32[1,18,1,128]{3,2,1,0:T(1,128)S(1)}, f32[1,18,1,128]{3,2,1,0:T(1,128)S(1)}, u32[]{:S(2)}, u32[]{:S(2)}) collective-permute-start(f32[1,18,1,128]{3,2,1,0:T(1,128)S(1)} %get-tuple-element.64), channel_id=1, source_target_pairs={{1,0},{2,1},{3,2},{4,3},{5,4},{6,5},{7,6},{8,7},{9,8},{10,9},{11,1... | collective-permute-start | bytes 27656 | tf_op jit(solution)/shard_map/ppermute | solution.py:17
  211.6 162.9 %collective-permute-start.5 = (f32[1,18,1,128]{3,2,1,0:T(1,128)S(1)}, f32[1,18,1,128]{3,2,1,0:T(1,128)S(1)}, u32[]{:S(2)}, u32[]{:S(2)}) collective-permute-start(f32[1,18,1,128]{3,2,1,0:T(1,128)S(1)} %get-tuple-element.65), channel_id=1, source_target_pairs={{0,1},{1,2},{2,3},{3,4},{4,5},{5,6},{6,7},{7,8},{8,9},{9,10},{10,1... | collective-permute-start | bytes 27656 | tf_op jit(solution)/shard_map/ppermute | solution.py:14
  367.9 7.4 collective-permute-start.23
  372.5 8.9 collective-permute-start.22
  381.4 5.4 collective-permute-start.24
  382.7 4.8 collective-permute-start.25
  604.6 16.1 %collective-permute-start.27 = (f32[1,1,16,128]{3,2,1,0:T(8,128)S(1)}, f32[1,1,16,128]{3,2,1,0:T(8,128)S(1)}, u32[]{:S(2)}, u32[]{:S(2)}) collective-permute-start(f32[1,1,16,128]{3,2,1,0:T(8,128)S(1)} %get-tuple-element.84), channel_id=1, source_target_pairs={{0,32},{32,64},{64,96},{96,128},{128,160},{160,192},{192,224},{224... | collective-permute-start | bytes 24584 | tf_op jit(solution)/shard_map/ppermute | solution.py:14
  609.2 11.5 collective-permute-start.26
  611.2 14.8 %collective-permute-start.7 = (f32[1,1,16,128]{3,2,1,0:T(8,128)S(1)}, f32[1,1,16,128]{3,2,1,0:T(8,128)S(1)}, u32[]{:S(2)}, u32[]{:S(2)}) collective-permute-start(f32[1,1,16,128]{3,2,1,0:T(8,128)S(1)} %get-tuple-element.80), channel_id=1, source_target_pairs={{0,32},{32,64},{64,96},{96,128},{128,160},{160,192},{192,224},{224... | collective-permute-start | bytes 24584 | tf_op jit(solution)/shard_map/ppermute | solution.py:14
  618.8 8.9 collective-permute-start.6
  620.8 12.2 collective-permute-start.28
  622.1 10.9 collective-permute-start.29
  627.7 6.1 collective-permute-start.8
  629.0 4.8 collective-permute-start.9
  853.9 6.9 collective-permute-start.11
  858.9 8.9 collective-permute-start.10
  867.8 5.4 collective-permute-start.12
  869.1 4.8 collective-permute-start.13
  1088.7 16.5 %collective-permute-start.31 = (f32[1,1,16,128]{3,2,1,0:T(8,128)S(1)}, f32[1,1,16,128]{3,2,1,0:T(8,128)S(1)}, u32[]{:S(2)}, u32[]{:S(2)}) collective-permute-start(f32[1,1,16,128]{3,2,1,0:T(8,128)S(1)} %get-tuple-element.68), channel_id=1, source_target_pairs={{0,32},{32,64},{64,96},{96,128},{128,160},{160,192},{192,224},{224... | collective-permute-start | bytes 24584 | tf_op jit(solution)/shard_map/ppermute | solution.py:14
  1093.7 11.5 collective-permute-start.30
  1095.7 14.8 %collective-permute-start.15 = (f32[1,1,16,128]{3,2,1,0:T(8,128)S(1)}, f32[1,1,16,128]{3,2,1,0:T(8,128)S(1)}, u32[]{:S(2)}, u32[]{:S(2)}) collective-permute-start(f32[1,1,16,128]{3,2,1,0:T(8,128)S(1)} %get-tuple-element.74), channel_id=1, source_target_pairs={{0,32},{32,64},{64,96},{96,128},{128,160},{160,192},{192,224},{224... | collective-permute-start | bytes 24584 | tf_op jit(solution)/shard_map/ppermute | solution.py:14
  1103.3 8.9 collective-permute-start.14
  1105.3 12.2 collective-permute-start.32
  1106.6 10.9 collective-permute-start.33
  1112.2 6.1 collective-permute-start.16
  1113.5 4.8 collective-permute-start.17
  1241.6 10.6 copy-start
  1241.7 10.5 copy-start.1
  1241.9 4.5 collective-permute-start.35
  1243.2 9.0 collective-permute-start.34
